TPU v7x, 32 devices: a whole 2x2x4 slice. The times are simulated.
32 devices in a mesh: grp: 4 (over x, core), seq: 8 (over z, y).
Axes of the slice: x: 2, y: 2, z: 4, core: 2. Of those that a mesh axis runs over, the one named last changes fastest.
Arguments:
- cand_queries: bfloat16 [4096, 128, 128], P(('grp', 'seq')), may hold values from -256 to 256
- candidate_keys: bfloat16 [512, 128, 128], P(('grp', 'seq')), may hold values from -6 to 6
- candidate_values: bfloat16 [512, 128, 128], P(('grp', 'seq')), may hold values from -24 to 24
- prefix_rotated_keys: bfloat16 [128, 1024], P(('grp', 'seq')), may hold values from -6.1 to 6.1
- prefix_value_matrix: bfloat16 [128, 1024], P(('grp', 'seq')), may hold values from -24 to 24
- lengths: int32 [64], replicated, may hold values from 32 to 128
Outputs:
- attended: bfloat16 [4096, 128, 128], P(('grp', 'seq'))
All inputs are finite; a program needn't handle non-finite values.
Results may differ from a plain program's by a relative error of at most 0.0076.
Values may be sent and summed in bfloat16 or wider, within the bound.
No kernel may reach another device: no remote copies, remote signals or barrier semaphores. Data moves between devices by JAX's collectives and lax.ppermute only.
A program may use at most 64 MiB of HBM per device.

v0:
```python
import math
import jax
import jax.numpy as jnp
import numpy as np
from jax import lax
from jax.sharding import PartitionSpec as P

QUERY_HEADS = 64
KEY_VALUE_HEADS = 8
HEAD_WIDTH = 128
rope_base = 500000.0


def rotate(vectors, positions):
    half_width = vectors.shape[-1] // 2
    exponents = jnp.arange(half_width, dtype=jnp.float32) * (2.0 / vectors.shape[-1])
    frequency = 1.0 / jnp.power(jnp.float32(rope_base), exponents)
    angles = positions.astype(jnp.float32)[:, None] * frequency[None, :]
    cosine = jnp.cos(angles)
    sine_table = jnp.sin(angles)
    lower_half = vectors[..., :half_width]
    upper_half = vectors[..., half_width:]
    return jnp.concatenate(
        [
            lower_half * cosine - upper_half * sine_table,
            upper_half * cosine + lower_half * sine_table,
        ],
        axis=-1,
    )


def pick_heads(key_row_list, value_row_list, head_table, sequence_count):
    row_total = key_row_list.shape[0]
    stacked = jnp.stack(
        [
            key_row_list.reshape(row_total, KEY_VALUE_HEADS, HEAD_WIDTH),
            value_row_list.reshape(row_total, KEY_VALUE_HEADS, HEAD_WIDTH),
        ],
        axis=2,
    )
    picked = jnp.take(stacked, head_table, axis=1)
    return picked.reshape(row_total, sequence_count, -1).transpose(1, 0, 2)


def shards(
    cand_queries,
    candidate_keys,
    candidate_values,
    prefix_rotated_keys,
    prefix_value_matrix,
    lengths,
):
    sequence_count = lax.axis_size("seq")
    grp_count = lax.axis_size("grp")
    head_rows = cand_queries.shape[0]
    cand_length = cand_queries.shape[1]
    key_value_rows = candidate_keys.shape[0]
    group_width = QUERY_HEADS // KEY_VALUE_HEADS
    key_value_heads = min(KEY_VALUE_HEADS, key_value_rows)
    prefix_here = prefix_rotated_keys.shape[0]
    prefix_total = prefix_here * sequence_count * grp_count
    score_scale = 1.0 / math.sqrt(HEAD_WIDTH)
    prefix_pick = (
        (np.arange(sequence_count)[:, None] * key_value_rows + np.arange(key_value_heads)[None, :])
        % KEY_VALUE_HEADS
    ).reshape(-1)
    outgoing = pick_heads(prefix_rotated_keys, prefix_value_matrix, prefix_pick, sequence_count)
    spread = lax.all_to_all(outgoing, "seq", split_axis=0, concat_axis=1, tiled=True)
    prefix_pair = lax.all_gather(spread, "grp", axis=1, tiled=True)
    prefix_pair = prefix_pair.reshape(prefix_total, key_value_heads, 2, HEAD_WIDTH)
    kv_table = np.arange(key_value_rows) % key_value_heads
    prefix_key_rows = jnp.take(prefix_pair[:, :, 0], kv_table, axis=1).transpose(1, 0, 2)
    prefix_value_rows = jnp.take(prefix_pair[:, :, 1], kv_table, axis=1).transpose(1, 0, 2)
    positions = prefix_total + jnp.arange(cand_length, dtype=jnp.int32)
    new_keys = rotate(candidate_keys.astype(jnp.float32), positions).astype(jnp.bfloat16)
    rotated = rotate(cand_queries.astype(jnp.float32), positions).astype(jnp.bfloat16)
    rotated = rotated.reshape(key_value_rows, group_width * cand_length, HEAD_WIDTH)
    all_keys = jnp.concatenate([prefix_key_rows, new_keys], axis=1)
    all_values = jnp.concatenate([prefix_value_rows, candidate_values], axis=1)
    key_count = prefix_total + cand_length
    block_rows = math.gcd(key_count, 512)
    block_count = key_count // block_rows
    row_total = group_width * cand_length
    row_token = jnp.arange(row_total, dtype=jnp.int32) % cand_length
    starts = jnp.arange(block_count, dtype=jnp.int32) * block_rows

    def attend(carry, block):
        maxima, totals, weighted = carry
        block_keys, block_values, first_row = block
        scores = (
            jnp.einsum("krd,knd->krn", rotated, block_keys, preferred_element_type=jnp.float32)
            * score_scale
        )
        cand_offset = first_row + jnp.arange(block_rows, dtype=jnp.int32) - prefix_total
        scores = jnp.where((cand_offset[None, :] <= row_token[:, None])[None], scores, -jnp.inf)
        highest = jnp.maximum(maxima, jnp.max(scores, axis=-1))
        decline = jnp.exp(maxima - highest)
        exponent = jnp.exp(scores - highest[..., None])
        totals = totals * decline + jnp.sum(exponent, axis=-1)
        weighted = weighted * decline[..., None] + jnp.einsum(
            "krn,knd->krd",
            exponent.astype(jnp.bfloat16),
            block_values,
            preferred_element_type=jnp.float32,
        )
        return ((highest, totals, weighted), None)

    start_state = (
        jnp.full((key_value_rows, row_total), -1e30, jnp.float32),
        jnp.zeros((key_value_rows, row_total), jnp.float32),
        jnp.zeros((key_value_rows, row_total, HEAD_WIDTH), jnp.float32),
    )
    key_blocks = all_keys.reshape(key_value_rows, block_count, block_rows, HEAD_WIDTH).transpose(
        1, 0, 2, 3
    )
    value_blocks = all_values.reshape(
        key_value_rows, block_count, block_rows, HEAD_WIDTH
    ).transpose(1, 0, 2, 3)
    final_state, unused = lax.scan(attend, start_state, (key_blocks, value_blocks, starts))
    maxima, totals, weighted = final_state
    attended = (weighted / totals[..., None]).reshape(head_rows, cand_length, HEAD_WIDTH)
    device_place = lax.axis_index("grp") * sequence_count + lax.axis_index("seq")
    cand_of_row = (device_place * head_rows + jnp.arange(head_rows, dtype=jnp.int32)) // QUERY_HEADS
    cand_slots = jnp.arange(lengths.shape[0], dtype=jnp.int32)
    cand_limit = jnp.sum(
        jnp.where(cand_of_row[:, None] == cand_slots[None, :], lengths[None, :], 0), axis=1
    )
    visible = jnp.arange(cand_length, dtype=jnp.int32)[None, :] < cand_limit[:, None]
    return jnp.where(visible[:, :, None], attended, jnp.float32(0.0)).astype(jnp.bfloat16)


def solution(mesh):
    return jax.shard_map(
        shards,
        mesh=mesh,
        in_specs=(
            P(("grp", "seq"), None, None),
            P(("grp", "seq"), None, None),
            P(("grp", "seq"), None, None),
            P(("grp", "seq"), None),
            P(("grp", "seq"), None),
            P(),
        ),
        out_specs=P(("grp", "seq"), None, None),
        check_vma=False,
    )
```

profile of v0, /device:TPU:0, one launch (start us, length us, event | category | flops | bytes accessed | tf_op | source)
XLA Modules:
  0.0 70.8 jit_solution(9848074302536593648)
XLA Ops:
  0.0 0.0 copy-start
  0.0 0.7 %pad_clamp_fusion.1 = s32[1024]{0:T(1024)S(1)} fusion(s32[64]{0:T(128)} %constant.134), kind=kLoop, calls=%fused_computation.44 | loop fusion | flops 1024 | bytes 4352 | tf_op jit(solution)/shard_map/jit(_take)/gather | solution.py:41
  0.7 0.7 %pad_maximum_fusion = bf16[4,8,2,128]{3,0,2,1:T(4,128)(2,1)S(1)} fusion(bf16[4,8,1,128]{3,0,2,1:T(4,128)(2,1)} %bitcast.24, bf16[4,8,1,128]{3,0,2,1:T(4,128)(2,1)} %bitcast.25), kind=kLoop, calls=%fused_computation.41 | loop fusion | flops 8192 | bytes 32768 | tf_op jit(solution)/shard_map/stack | solution.py:34
  1.5 0.7 gather_fusion
  2.1 0.1 copy.24
  2.3 0.1 gather.10
  2.3 0.8 %copy.25 = bf16[8,4,2048]{2,1,0:T(4,128)(2,1)} copy(bf16[8,4,2048]{2,0,1:T(8,128)(2,1)S(1)} %bitcast.23) | data formatting | bytes 262144 | tf_op jit(solution)/shard_map/transpose | solution.py:42
  3.1 7.3 %all-to-all-start = ((bf16[8,4,2048]{2,1,0:T(4,128)(2,1)}), bf16[8,4,2048]{2,1,0:T(4,128)(2,1)S(1)}, u32[]{:S(2)}, u32[]{:S(2)}) async-start(bf16[8,4,2048]{2,1,0:T(4,128)(2,1)} %copy.25), calls=%async_computation | async-start | bytes 262144 | tf_op jit(solution)/shard_map/all_to_all | solution.py:68
  10.5 3.2 %convert_element_type.38 = f32[128,128,128]{2,1,0:T(8,128)S(1)} convert(bf16[128,128,128]{2,1,0:T(8,128)(2,1)} %param.10) | non-fusion elementwise | flops 2097152 | bytes 12582912 | tf_op jit(solution)/shard_map/convert_element_type | solution.py:76
  13.7 0.0 copy-done
  13.7 0.1 convert_element_type.40
  13.8 0.3 multiply_cosine_fusion
  14.1 0.0 copy-start.1
  14.2 0.0 copy-start.3
  14.2 5.0 %subtract_convert_fusion = (bf16[128,128,64]{2,1,0:T(8,128)(2,1)}, bf16[128,128,64]{2,1,0:T(8,128)(2,1)}) fusion(f32[128,128,128]{2,1,0:T(8,128)S(1)} %convert_element_type.38, f32[128,64]{1,0:T(8,128)S(1)} %get-tuple-element.39, f32[128,64]{1,0:T(8,128)S(1)} %get-tuple-element.38), kind=kLoop, calls=%fused_computation.15 | loop fusion | flops 8388608 | bytes 12648448 | tf_op jit(solution)/shard_map/convert.5
  19.2 0.4 subtract_convert_fusion.1
  19.6 0.0 copy-done.1
  19.7 0.0 copy-done.3
  19.7 0.1 select_reduce_fusion
  19.8 0.1 iota_compare_fusion
  19.9 0.2 broadcast_compare_fusion
  20.1 0.0 all-to-all-done
  20.1 7.2 %all_gather.3 = bf16[1,128,2048]{2,1,0:T(8,128)(2,1)S(1)} all-gather(bf16[1,32,2048]{2,1,0:T(8,128)(2,1)S(1)} %all_to_all.10), channel_id=1, replica_groups=mesh['grp'=4,'seq'=8] {'grp'}, dimensions={1}, use_global_device_ids=true | all-gather | bytes 655360 | tf_op jit(solution)/shard_map/all_gather | solution.py:69
  27.3 0.4 reshape.191
  27.7 0.7 %fusion.31 = (bf16[128,8,1,128]{3,2,1,0:T(2,128)(2,1)S(1)}, bf16[128,8,1,128]{3,2,1,0:T(2,128)(2,1)S(1)}) fusion(bf16[128,8,2,128]{3,2,1,0:T(2,128)(2,1)S(1)} %reshape.191), kind=kLoop, calls=%fused_computation.61 | loop fusion | bytes 1048576 | tf_op jit(solution)/shard_map/slice | solution.py:73
  28.4 0.2 copy_bitcast_fusion
  28.6 0.6 gather_fusion.1
  29.3 15.3 %fusion = (f32[16,1024]{1,0:T(8,128)S(1)}, f32[16,1024,256]{1,2,0:T(8,128)}) fusion(pred[1024,256]{0,1:T(8,128)(4,1)S(1)} %broadcast_compare_fusion, bf16[16,128,64]{2,1,0:T(8,128)(2,1)S(1)} %get-tuple-element.23, bf16[16,128,64]{2,1,0:T(8,128)(2,1)S(1)} %get-tuple-element.22, bf16[16,128,128]{2,1,0:T(8,128)(2,1)S(1)} %gather_fusion.1, ...), kind=kOutput, calls=%fused_computation.5 | convolution fusion | flops 1097842688 | bytes 22347776 | tf_op jit(solution)/shard_map/while/body/eval_jaxpr/krd,knd->krn/dot_general | solution.py:91
  44.6 0.0 copy-start.2
  44.6 9.3 %fusion.1 = f32[16,1024]{1,0:T(8,128)S(1)} fusion(f32[16,1024,256]{1,2,0:T(8,128)} %get-tuple-element.41, f32[16,1024]{1,0:T(8,128)S(1)} %broadcast_maximum_fusion, pred[1024,256]{0,1:T(8,128)(4,1)S(1)} %broadcast_compare_fusion), kind=kLoop, calls=%fused_computation.6 | loop fusion | flops 16760832 | bytes 17170432 | tf_op jit(solution)/shard_map/while/body/eval_jaxpr/reduce_sum | solution.py:99
  53.9 0.6 gather_fusion.2
  54.5 0.0 copy-done.2
  54.5 11.3 %add_divide_fusion = bf16[16,1024,128]{2,1,0:T(8,128)(2,1)S(1)} fusion(f32[16,1024]{1,0:T(8,128)S(1)} %get-tuple-element.37, f32[16,1024]{1,0:T(8,128)S(1)} %get-tuple-element.36, f32[16,1024,256]{1,2,0:T(8,128)} %get-tuple-element.41, f32[16,1024]{1,0:T(8,128)S(1)} %broadcast_maximum_fusion, pred[1024,256]{0,1:T(8,128)(4,1)S(1)} %broadcast_compare_fusion, ...), kind=kOutput, calls=%fused_computation.10 | convolution fusion | flops 1098907648 | bytes 22478848 | tf_op jit(solution)/shard_map/while/body/eval_jaxpr/krn,knd->krd/dot_general | solution.py:100
  65.9 4.9 %select_convert_fusion = bf16[128,128,128]{2,1,0:T(8,128)(2,1)} fusion(bf16[128,128,128]{2,1,0:T(8,128)(2,1)S(1)} %bitcast.21, pred[128,128]{1,0:T(8,128)(4,1)S(1)} %iota_compare_fusion), kind=kLoop, calls=%fused_computation.9 | loop fusion | flops 2097152 | bytes 8404992 | tf_op jit(solution)/shard_map/convert_element_type | solution.py:129
  (9 shorter events, 0.1 us)
Async XLA Ops:
  0.0 13.7 %copy-start = (bf16[16,128,128]{2,1,0:T(8,128)(2,1)S(1)}, bf16[16,128,128]{2,1,0:T(8,128)(2,1)}, u32[]{:S(2)}) copy-start(bf16[16,128,128]{2,1,0:T(8,128)(2,1)} %param.11) | copy-start | bytes 1572868
  3.1 17.0 %all-to-all-start = ((bf16[8,4,2048]{2,1,0:T(4,128)(2,1)}), bf16[8,4,2048]{2,1,0:T(4,128)(2,1)S(1)}, u32[]{:S(2)}, u32[]{:S(2)}) async-start(bf16[8,4,2048]{2,1,0:T(4,128)(2,1)} %copy.25), calls=%async_computation | async-start | bytes 262144 | tf_op jit(solution)/shard_map/all_to_all | solution.py:68
  14.1 5.5 %copy-start.1 = (s32[16]{0:T(128)S(1)}, s32[16]{0:T(128)}, u32[]{:S(2)}) copy-start(s32[16]{0:T(128)} %constant.137) | copy-start | bytes 196
  14.2 5.5 %copy-start.3 = (s32[64]{0:T(128)S(1)}, s32[64]{0:T(128)}, u32[]{:S(2)}) copy-start(s32[64]{0:T(128)} %param.15) | copy-start | bytes 772
  44.6 10.0 %copy-start.2 = (bf16[16,128,128]{2,1,0:T(8,128)(2,1)S(1)}, bf16[16,128,128]{2,1,0:T(8,128)(2,1)}, u32[]{:S(2)}) copy-start(bf16[16,128,128]{2,1,0:T(8,128)(2,1)} %param.12) | copy-start | bytes 1572868
where the time goes:
time: 71.2 us; the launch traced here: 70.8 us
  matrix products  26.6 us (37%)
  other arithmetic  25.2 us (35%)
  starting transfers between devices  7.31 us (10%)
  blocking collectives  7.17 us (10%)
  local copies, waits for them, and re-layouts  4.28 us (6%)
    dot_general x1, matrix products, attend(): jnp.einsum('krd,knd->krn', rotated, block_keys, preferred_element_type=jn...  15.3 us
    dot_general x1, matrix products, attend(): jnp.einsum('krn,knd->krd', exponent.astype(jnp.bfloat16), block_values, p...  11.3 us
    reduce_sum x1, other arithmetic, attend(): totals = totals * decline + jnp.sum(exponent, axis=-1)  9.26 us
    all_to_all x1, starting transfers between devices, shards(): lax.all_to_all(outgoing, 'seq', split_axis=0, concat_axis=1, tiled=True)  7.31 us
    all_gather x1, blocking collectives, shards(): prefix_pair = lax.all_gather(spread, 'grp', axis=1, tiled=True)  7.17 us
    another operation x2, other arithmetic  5.46 us
    convert_element_type x1, other arithmetic, shards(): jnp.where(visible[:, :, None], attended, jnp.float32(0.0))  4.9 us
    convert_element_type x1, other arithmetic, shards(): cand_queries.astype(jnp.float32)  3.25 us
  transfers between devices with their start and end apart: 1, of which 0 were waited for; matrix products, arithmetic and copies ran while one was open for 13% of the time, Pallas kernels for 0%

commit v1 on v0

--- a/solution.py
+++ b/solution.py
@@ -66,7 +66,12 @@
     ).reshape(-1)
     outgoing = pick_heads(prefix_rotated_keys, prefix_value_matrix, prefix_pick, sequence_count)
     spread = lax.all_to_all(outgoing, "seq", split_axis=0, concat_axis=1, tiled=True)
-    prefix_pair = lax.all_gather(spread, "grp", axis=1, tiled=True)
+    ring = [spread]
+    for hop in range(3):
+        ring.append(lax.ppermute(ring[-1], "grp", [(dev, (dev + 1) % 4) for dev in range(4)]))
+    prefix_pair = jnp.roll(
+        jnp.concatenate(ring[::-1], axis=1), (lax.axis_index("grp") + 1) * ring[0].shape[1], axis=1
+    )
     prefix_pair = prefix_pair.reshape(prefix_total, key_value_heads, 2, HEAD_WIDTH)
     kv_table = np.arange(key_value_rows) % key_value_heads
     prefix_key_rows = jnp.take(prefix_pair[:, :, 0], kv_table, axis=1).transpose(1, 0, 2)

time: 71.2 us -> 83.8 us (1.18)
  waiting for transfers between devices: 0.01 us -> 12.7 us
  other arithmetic: 25.2 us -> 32.9 us
  blocking collectives: 7.17 us -> 0 us
    ppermute x0 -> x3, waiting for transfers between devices: none -> 12.7 us  [shards(): lax.ppermute(ring[-1], 'grp', [(dev, (dev + 1) % 4) for dev in range(4)])]
    all_gather x1 -> x0, blocking collectives: 7.17 us -> none  [shards(): prefix_pair = lax.all_gather(spread, 'grp', axis=1, tiled=True)]
    another operation x2, other arithmetic: 5.46 us -> 9.9 us
    convert_element_type x1, other arithmetic: 3.25 us -> 6.48 us  [shards(): cand_queries.astype(jnp.float32)]
  transfers between devices with their start and end apart: 1 -> 4, of which waited for: 0 -> 3; matrix products, arithmetic and copies ran while one was open for 13% -> 21% of each run, Pallas kernels for 0% -> 0%
where the time goes in v1:
time: 83.8 us; the launch traced here: 83.4 us
  other arithmetic  32.9 us (39%)
  matrix products  26.4 us (32%)
  waiting for transfers between devices  12.7 us (15%)
  starting transfers between devices  7.37 us (9%)
  local copies, waits for them, and re-layouts  3.78 us (5%)
    dot_general x1, matrix products, attend(): jnp.einsum('krd,knd->krn', rotated, block_keys, preferred_element_type=jn...  15.1 us
    ppermute x3, waiting for transfers between devices, shards(): lax.ppermute(ring[-1], 'grp', [(dev, (dev + 1) % 4) for dev in range(4)])  12.7 us
    dot_general x1, matrix products, attend(): jnp.einsum('krn,knd->krd', exponent.astype(jnp.bfloat16), block_values, p...  11.3 us
    another operation x2, other arithmetic  9.9 us
    reduce_sum x1, other arithmetic, attend(): totals = totals * decline + jnp.sum(exponent, axis=-1)  9.26 us
    all_to_all x1, starting transfers between devices, shards(): lax.all_to_all(outgoing, 'seq', split_axis=0, concat_axis=1, tiled=True)  7.31 us
    convert_element_type x1, other arithmetic, shards(): cand_queries.astype(jnp.float32)  6.48 us
    convert_element_type x1, other arithmetic, shards(): jnp.where(visible[:, :, None], attended, jnp.float32(0.0))  4.9 us
  transfers between devices with their start and end apart: 4, of which 3 were waited for; matrix products, arithmetic and copies ran while one was open for 21% of the time, Pallas kernels for 0%

profile of v1, /device:TPU:0, one launch (start us, length us, event | category | flops | bytes accessed | tf_op | source)
XLA Modules:
  0.0 83.4 jit_solution(10905010736911138128)
XLA Ops:
  0.0 0.0 copy-start
  0.0 0.7 pad_clamp_fusion
  0.7 0.7 pad_maximum_fusion
  1.5 0.7 gather_fusion
  2.2 0.1 copy.31
  2.3 0.1 gather.10
  2.4 0.8 copy.32
  3.1 7.3 %all-to-all-start = ((bf16[8,4,2048]{2,1,0:T(4,128)(2,1)}), bf16[8,4,2048]{2,1,0:T(4,128)(2,1)S(1)}, u32[]{:S(2)}, u32[]{:S(2)}) async-start(bf16[8,4,2048]{2,1,0:T(4,128)(2,1)} %copy.32), calls=%async_computation | async-start | bytes 262144 | tf_op jit(solution)/shard_map/all_to_all | solution.py:68
  10.5 6.5 %convert_element_type.38 = f32[128,128,128]{2,1,0:T(8,128)} convert(bf16[128,128,128]{2,1,0:T(8,128)(2,1)} %param.10) | non-fusion elementwise | flops 2097152 | bytes 12582912 | tf_op jit(solution)/shard_map/convert_element_type | solution.py:81
  17.0 0.0 copy-done
  17.0 0.1 convert_element_type.40
  17.1 0.3 multiply_cosine_fusion
  17.4 0.0 copy-start.2
  17.4 9.5 %subtract_convert_fusion = (bf16[128,128,64]{2,1,0:T(8,128)(2,1)}, bf16[128,128,64]{2,1,0:T(8,128)(2,1)}) fusion(f32[128,128,128]{2,1,0:T(8,128)} %convert_element_type.38, f32[128,64]{1,0:T(8,128)S(1)} %get-tuple-element.39, f32[128,64]{1,0:T(8,128)S(1)} %get-tuple-element.38), kind=kLoop, calls=%fused_computation.15 | loop fusion | flops 8388608 | bytes 12648448 | tf_op jit(solution)/shard_map/convert.5
  26.9 0.4 subtract_convert_fusion.1
  27.3 0.0 all-to-all-done
  27.4 0.1 collective-permute-start
  27.4 0.2 broadcast_compare_fusion
  27.6 4.2 %collective-permute-done = bf16[1,32,2048]{2,1,0:T(8,128)(2,1)S(1)} collective-permute-done((bf16[1,32,2048]{2,1,0:T(8,128)(2,1)S(1)}, bf16[1,32,2048]{2,1,0:T(8,128)(2,1)S(1)}, u32[]{:S(2)}, u32[]{:S(2)}) %collective-permute-start) | collective-permute-done | bytes 131104 | tf_op jit(solution)/shard_map/ppermute | solution.py:71
  31.8 0.0 collective-permute-start.1
  31.8 0.0 copy-done.2
  31.8 0.1 select_reduce_fusion
  31.9 4.3 %collective-permute-done.1 = bf16[1,32,2048]{2,1,0:T(8,128)(2,1)S(1)} collective-permute-done((bf16[1,32,2048]{2,1,0:T(8,128)(2,1)S(1)}, bf16[1,32,2048]{2,1,0:T(8,128)(2,1)S(1)}, u32[]{:S(2)}, u32[]{:S(2)}) %collective-permute-start.1) | collective-permute-done | bytes 131104 | tf_op jit(solution)/shard_map/ppermute | solution.py:71
  36.2 0.0 collective-permute-start.2
  36.2 0.1 iota_compare_fusion
  36.3 4.3 %collective-permute-done.2 = bf16[1,32,2048]{2,1,0:T(8,128)(2,1)S(1)} collective-permute-done((bf16[1,32,2048]{2,1,0:T(8,128)(2,1)S(1)}, bf16[1,32,2048]{2,1,0:T(8,128)(2,1)S(1)}, u32[]{:S(2)}, u32[]{:S(2)}) %collective-permute-start.2) | collective-permute-done | bytes 131104 | tf_op jit(solution)/shard_map/ppermute | solution.py:71
  40.8 0.3 copy.33
  41.1 0.2 copy.35
  41.3 0.7 gather_fusion.1
  42.0 15.1 %fusion = (f32[16,1024]{1,0:T(8,128)S(1)}, f32[16,1024,256]{1,2,0:T(8,128)}) fusion(pred[1024,256]{0,1:T(8,128)(4,1)S(1)} %broadcast_compare_fusion, bf16[16,128,64]{2,1,0:T(8,128)(2,1)S(1)} %get-tuple-element.23, bf16[16,128,64]{2,1,0:T(8,128)(2,1)S(1)} %get-tuple-element.22, bf16[16,128,128]{2,1,0:T(8,128)(2,1)S(1)} %gather_fusion.1, ...), kind=kOutput, calls=%fused_computation.5 | convolution fusion | flops 1097842688 | bytes 22347776 | tf_op jit(solution)/shard_map/while/body/eval_jaxpr/krd,knd->krn/dot_general | solution.py:96
  57.0 0.0 copy-start.1
  57.0 9.3 %fusion.1 = f32[16,1024]{1,0:T(8,128)S(1)} fusion(f32[16,1024,256]{1,2,0:T(8,128)} %get-tuple-element.41, f32[16,1024]{1,0:T(8,128)S(1)} %broadcast_maximum_fusion, pred[1024,256]{0,1:T(8,128)(4,1)S(1)} %broadcast_compare_fusion), kind=kLoop, calls=%fused_computation.6 | loop fusion | flops 16760832 | bytes 17170432 | tf_op jit(solution)/shard_map/while/body/eval_jaxpr/reduce_sum | solution.py:104
  66.3 0.2 copy.37
  66.5 0.7 gather_fusion.2
  67.2 0.0 copy-done.1
  67.2 11.3 %add_divide_fusion = bf16[16,1024,128]{2,1,0:T(8,128)(2,1)S(1)} fusion(f32[16,1024]{1,0:T(8,128)S(1)} %get-tuple-element.37, f32[16,1024]{1,0:T(8,128)S(1)} %get-tuple-element.36, f32[16,1024,256]{1,2,0:T(8,128)} %get-tuple-element.41, f32[16,1024]{1,0:T(8,128)S(1)} %broadcast_maximum_fusion, pred[1024,256]{0,1:T(8,128)(4,1)S(1)} %broadcast_compare_fusion, ...), kind=kOutput, calls=%fused_computation.10 | convolution fusion | flops 1098907648 | bytes 22478848 | tf_op jit(solution)/shard_map/while/body/eval_jaxpr/krn,knd->krd/dot_general | solution.py:105
  78.5 4.9 %select_convert_fusion = bf16[128,128,128]{2,1,0:T(8,128)(2,1)} fusion(bf16[128,128,128]{2,1,0:T(8,128)(2,1)S(1)} %bitcast.20, pred[128,128]{1,0:T(8,128)(4,1)S(1)} %iota_compare_fusion), kind=kLoop, calls=%fused_computation.9 | loop fusion | flops 2097152 | bytes 8404992 | tf_op jit(solution)/shard_map/convert_element_type | solution.py:134
  (18 shorter events, 0.3 us)
Async XLA Ops:
  0.0 17.0 %copy-start = (bf16[16,128,128]{2,1,0:T(8,128)(2,1)S(1)}, bf16[16,128,128]{2,1,0:T(8,128)(2,1)}, u32[]{:S(2)}) copy-start(bf16[16,128,128]{2,1,0:T(8,128)(2,1)} %param.11) | copy-start | bytes 1572868
  3.1 24.2 %all-to-all-start = ((bf16[8,4,2048]{2,1,0:T(4,128)(2,1)}), bf16[8,4,2048]{2,1,0:T(4,128)(2,1)S(1)}, u32[]{:S(2)}, u32[]{:S(2)}) async-start(bf16[8,4,2048]{2,1,0:T(4,128)(2,1)} %copy.32), calls=%async_computation | async-start | bytes 262144 | tf_op jit(solution)/shard_map/all_to_all | solution.py:68
  17.4 14.4 %copy-start.2 = (s32[64]{0:T(128)S(1)}, s32[64]{0:T(128)}, u32[]{:S(2)}) copy-start(s32[64]{0:T(128)} %param.15) | copy-start | bytes 772
  27.4 4.4 %collective-permute-start = (bf16[1,32,2048]{2,1,0:T(8,128)(2,1)S(1)}, bf16[1,32,2048]{2,1,0:T(8,128)(2,1)S(1)}, u32[]{:S(2)}, u32[]{:S(2)}) collective-permute-start(bf16[1,32,2048]{2,1,0:T(8,128)(2,1)S(1)} %all_to_all.10), channel_id=1, source_target_pairs={{0,8},{8,16},{16,24},{24,0},{1,9},{9,17},{17,25},{25,1},{2,10},{10... | collective-permute-start | bytes 393224 | tf_op jit(solution)/shard_map/ppermute | solution.py:71
  31.8 4.4 %collective-permute-start.1 = (bf16[1,32,2048]{2,1,0:T(8,128)(2,1)S(1)}, bf16[1,32,2048]{2,1,0:T(8,128)(2,1)S(1)}, u32[]{:S(2)}, u32[]{:S(2)}) collective-permute-start(bf16[1,32,2048]{2,1,0:T(8,128)(2,1)S(1)} %collective-permute-done), channel_id=1, source_target_pairs={{0,8},{8,16},{16,24},{24,0},{1,9},{9,17},{17,25},{25,1},{2,10},{10... | collective-permute-start | bytes 393224 | tf_op jit(solution)/shard_map/ppermute | solution.py:71
  36.2 4.4 %collective-permute-start.2 = (bf16[1,32,2048]{2,1,0:T(8,128)(2,1)S(1)}, bf16[1,32,2048]{2,1,0:T(8,128)(2,1)S(1)}, u32[]{:S(2)}, u32[]{:S(2)}) collective-permute-start(bf16[1,32,2048]{2,1,0:T(8,128)(2,1)S(1)} %collective-permute-done.1), channel_id=1, source_target_pairs={{0,8},{8,16},{16,24},{24,0},{1,9},{9,17},{17,25},{25,1},{2,10},{10... | collective-permute-start | bytes 393224 | tf_op jit(solution)/shard_map/ppermute | solution.py:71
  57.0 10.2 %copy-start.1 = (bf16[16,128,128]{2,1,0:T(8,128)(2,1)S(1)}, bf16[16,128,128]{2,1,0:T(8,128)(2,1)}, u32[]{:S(2)}) copy-start(bf16[16,128,128]{2,1,0:T(8,128)(2,1)} %param.12) | copy-start | bytes 1572868
